TPU v7x, 512 devices: a whole 4x4x16 slice. The times are simulated.
512 devices in a mesh: tm: 64 (over y, z), head: 8 (over x, core).
Axes of the slice: x: 4, y: 4, z: 16, core: 2. Of those that a mesh axis runs over, the one named last changes fastest.
Arguments:
- queries: bfloat16 [16384, 3072], P('tm', 'head'), may hold values from -170 to 170
- key_rows: bfloat16 [16384, 3072], P('tm', 'head'), may hold values from -6 to 6
- value_rows: bfloat16 [16384, 3072], P('tm', 'head'), may hold values from -102 to 102
- grad_normed: bfloat16 [16384, 3072], P('tm', 'head'), may hold values from -5.5 to 5.5
- norm_gain: float32 [3072], P('head'), may hold values from 0.25 to 1.75
- utter_ids: int32 [128], P('tm'), may hold values from 0 to 20, never falling along the last dimension, each value on 1 to 8 neighbouring positions
Outputs:
- normed: bfloat16 [16384, 3072], P('tm', 'head')
- grad_queries: bfloat16 [16384, 3072], P('tm', 'head')
- grad_keys: bfloat16 [16384, 3072], P('tm', 'head')
- grad_values: bfloat16 [16384, 3072], P('tm', 'head')
- grad_gain: float32 [3072], P('head')
Inputs may be any that keep to these rules, and one draw needn't show every extreme that they name: `utter_ids`: ids never fall; each utterance covers 1 to 8 consecutive blocks of 128 frames, and one covers exactly 8.
All inputs are finite; a program needn't handle non-finite values.
Results may differ from a plain program's by a relative error of at most 0.024.
Values may be sent and summed in bfloat16 or wider, within the bound.
A program may use at most 64 MiB of HBM per device.

v0:
```python
import jax
import jax.numpy as jnp
from jax import lax
from jax.sharding import PartitionSpec as P

HSZ = 128
REACH = 4


def for_sending(x):

    def short(part):
        return part.astype(jnp.bfloat16) if part.dtype == jnp.float32 else part

    return jax.tree.map(short, x)


def passed_along(x, axis, by):
    length = lax.axis_size(axis)
    pairs = [(i, i + by) for i in range(length) if 0 <= i + by < length]
    return lax.ppermute(x, axis, pairs)


def frame_utter(utter_ids, row_count):
    blocks = utter_ids.shape[0]
    spread = jnp.broadcast_to(utter_ids[:, None] + 1, (blocks, row_count // blocks))
    return spread.reshape(row_count)


def rounded_term(term):
    return lax.optimization_barrier(term.astype(jnp.bfloat16)).astype(jnp.float32)


def tile_scores(query_heads, key_heads, query_utt, key_utt, factor):
    scores = (
        jnp.einsum("qhe,khe->hqk", query_heads, key_heads, preferred_element_type=jnp.float32)
        * factor
    )
    allowed = query_utt[:, None] == key_utt[None, :]
    return jnp.where(allowed[None], scores, -jnp.inf)


def lse_step(query_heads, query_utt, key_heads, key_utt, factor, current):
    top_score, exp_total = current
    scores = tile_scores(query_heads, key_heads, query_utt, key_utt, factor)
    new_top = jnp.maximum(top_score, jnp.max(scores, axis=2))
    exp_total = exp_total * jnp.exp(top_score - new_top) + jnp.sum(
        jnp.exp(scores - new_top[:, :, None]), axis=2
    )
    return (new_top, exp_total)


def output_step(
    query_heads, query_utt, key_heads, value_heads, key_utt, log_total, factor, out_accum
):
    weights = jnp.exp(
        tile_scores(query_heads, key_heads, query_utt, key_utt, factor) - log_total[:, :, None]
    )
    return out_accum + jnp.einsum(
        "hqk,khe->qhe",
        weights.astype(jnp.bfloat16),
        value_heads,
        preferred_element_type=jnp.float32,
    )


def tile_grads(
    query_heads,
    grad_heads,
    key_heads,
    value_heads,
    query_utt,
    key_utt,
    log_total,
    row_delta,
    factor,
):
    scores = tile_scores(query_heads, key_heads, query_utt, key_utt, factor)
    weights = jnp.exp(scores - log_total[:, :, None])
    grad_weights = jnp.einsum(
        "qhe,khe->hqk", grad_heads, value_heads, preferred_element_type=jnp.float32
    )
    dscore = (weights * (grad_weights - row_delta[:, :, None])).astype(jnp.bfloat16)
    return (weights.astype(jnp.bfloat16), dscore)


def query_step(
    query_heads,
    grad_heads,
    key_heads,
    value_heads,
    query_utt,
    key_utt,
    log_total,
    row_delta,
    factor,
    current,
):
    weights_b, dscore = tile_grads(
        query_heads,
        grad_heads,
        key_heads,
        value_heads,
        query_utt,
        key_utt,
        log_total,
        row_delta,
        factor,
    )
    grad_query = (
        current[0]
        + jnp.einsum("hqk,khe->qhe", dscore, key_heads, preferred_element_type=jnp.float32) * factor
    )
    key_grad = (
        jnp.einsum("hqk,qhe->khe", dscore, query_heads, preferred_element_type=jnp.float32) * factor
    )
    value_grad = jnp.einsum(
        "hqk,qhe->khe", weights_b, grad_heads, preferred_element_type=jnp.float32
    )
    return (grad_query, key_grad, value_grad)


def body(queries, key_rows, value_rows, grad_normed, norm_gain, utter_ids):
    row_count, feat_width = queries.shape
    head_count = feat_width // HSZ
    factor = HSZ ** (-0.5)
    layout = (row_count, head_count, HSZ)
    query_heads = queries.reshape(layout)
    own_utt = frame_utter(utter_ids, row_count)
    own_pair = jnp.stack([key_rows, value_rows])
    sources = [(own_pair, own_utt)]
    moving = (own_pair, own_utt)
    for distance in range(REACH):
        moving = passed_along((moving[0], for_sending(moving[1])), "tm", 1)
        sources.append(moving)
    key_blocks = []
    for source in sources:
        pair_rows = source[0]
        key_utt = source[1]
        live = jnp.any(own_utt[:, None] == key_utt[None, :])
        key_blocks.append(
            (pair_rows[0].reshape(layout), pair_rows[1].reshape(layout), key_utt, live)
        )
    top_score = jnp.full((head_count, row_count), -jnp.inf, jnp.float32)
    exp_total = jnp.zeros((head_count, row_count), jnp.float32)
    for key_block in key_blocks:
        top_score, exp_total = lse_step(
            query_heads, own_utt, key_block[0], key_block[2], factor, (top_score, exp_total)
        )
    log_total = top_score + jnp.log(exp_total)
    out_accum = jnp.zeros(layout, jnp.float32)
    for key_block in key_blocks:
        out_accum = output_step(
            query_heads,
            own_utt,
            key_block[0],
            key_block[1],
            key_block[2],
            log_total,
            factor,
            out_accum,
        )
    attended = out_accum.astype(jnp.bfloat16)
    flat_att = attended.reshape(row_count, feat_width).astype(jnp.float32)
    features = feat_width * lax.axis_size("head")
    grad_rows = grad_normed.astype(jnp.float32)
    scaled = grad_rows * norm_gain
    square_sum, cross_sum = lax.psum(
        (jnp.sum(flat_att * flat_att, axis=1), jnp.sum(scaled * flat_att, axis=1)), "head"
    )
    rms_inv = 1.0 / jnp.sqrt(square_sum / features + 1e-06)
    normed = (flat_att * rms_inv[:, None] * norm_gain).astype(jnp.bfloat16)
    grad_att = (
        rms_inv[:, None] * (scaled - flat_att * (rms_inv * rms_inv * cross_sum / features)[:, None])
    ).astype(jnp.bfloat16)
    grad_gain = lax.psum(jnp.sum(grad_rows * flat_att * rms_inv[:, None], axis=0), "tm")
    grad_heads = grad_att.reshape(layout)
    row_delta = jnp.sum(attended.astype(jnp.float32) * grad_heads.astype(jnp.float32), axis=2).T
    zero_heads = jnp.zeros(layout, jnp.float32)
    grad_query = zero_heads
    key_parts = []
    for key_block in key_blocks:
        grad_query, key_grad, value_grad = query_step(
            query_heads,
            grad_heads,
            key_block[0],
            key_block[1],
            own_utt,
            key_block[2],
            log_total,
            row_delta,
            factor,
            (grad_query, zero_heads, zero_heads),
        )
        key_parts.append(
            jnp.stack(
                [key_grad.reshape(row_count, feat_width), value_grad.reshape(row_count, feat_width)]
            )
        )
    carried = rounded_term(key_parts[0])
    for distance in range(1, REACH + 1):
        arrived = passed_along(key_parts[distance].astype(jnp.bfloat16), "tm", -distance)
        carried = carried + arrived.astype(jnp.float32)
    grad_queries = grad_query.reshape(row_count, feat_width).astype(jnp.bfloat16)
    return (
        normed,
        grad_queries,
        carried[0].astype(jnp.bfloat16),
        carried[1].astype(jnp.bfloat16),
        grad_gain,
    )


def solution(mesh):
    in_specs = (
        P("tm", "head"),
        P("tm", "head"),
        P("tm", "head"),
        P("tm", "head"),
        P("head"),
        P("tm"),
    )
    out_specs = (P("tm", "head"), P("tm", "head"), P("tm", "head"), P("tm", "head"), P("head"))
    return jax.shard_map(body, mesh=mesh, in_specs=in_specs, out_specs=out_specs, check_vma=False)
```

profile of v0, /device:TPU:6, one launch (start us, length us, event | category | flops | bytes accessed | tf_op | source)
XLA Modules:
  0.0 350.9 jit_solution(14660419836064884476)
XLA Ops:
  1.4 3.9 %collective-permute-start = (s32[256]{0:T(256)S(1)}, s32[256]{0:T(256)S(1)}, u32[]{:S(2)}, u32[]{:S(2)}) collective-permute-start(s32[256]{0:T(256)S(1)} %broadcast_bitcast_fusion), channel_id=1, source_target_pairs={{0,8},{8,16},{16,24},{24,32},{32,40},{40,48},{48,56},{56,64},{64,7... | collective-permute-start | bytes 3080 | tf_op jit(solution)/shard_map/ppermute | solution.py:21
  5.3 1.3 collective-permute-done
  6.6 4.2 %collective-permute-start.2 = (s32[256]{0:T(256)S(1)}, s32[256]{0:T(256)S(1)}, u32[]{:S(2)}, u32[]{:S(2)}) collective-permute-start(s32[256]{0:T(256)S(1)} %collective-permute-done), channel_id=1, source_target_pairs={{0,8},{8,16},{16,24},{24,32},{32,40},{40,48},{48,56},{56,64},{64,7... | collective-permute-start | bytes 3080 | tf_op jit(solution)/shard_map/ppermute | solution.py:21
  10.8 1.3 collective-permute-done.2
  12.0 4.2 %collective-permute-start.4 = (s32[256]{0:T(256)S(1)}, s32[256]{0:T(256)S(1)}, u32[]{:S(2)}, u32[]{:S(2)}) collective-permute-start(s32[256]{0:T(256)S(1)} %collective-permute-done.2), channel_id=1, source_target_pairs={{0,8},{8,16},{16,24},{24,32},{32,40},{40,48},{48,56},{56,64},{64,7... | collective-permute-start | bytes 3080 | tf_op jit(solution)/shard_map/ppermute | solution.py:21
  16.2 1.1 copy.85
  17.5 4.3 %collective-permute-start.6 = (s32[256]{0:T(256)S(1)}, s32[256]{0:T(256)S(1)}, u32[]{:S(2)}, u32[]{:S(2)}) collective-permute-start(s32[256]{0:T(256)S(1)} %collective-permute-done.4), channel_id=1, source_target_pairs={{0,8},{8,16},{16,24},{24,32},{32,40},{40,48},{48,56},{56,64},{64,7... | collective-permute-start | bytes 3080 | tf_op jit(solution)/shard_map/ppermute | solution.py:21
  21.9 5.5 %collective-permute-start.1 = (bf16[2,256,384]{1,2,0:T(8,128)(2,1)S(1)}, bf16[2,256,384]{1,2,0:T(8,128)(2,1)S(1)}, u32[]{:S(2)}, u32[]{:S(2)}) collective-permute-start(bf16[2,256,384]{1,2,0:T(8,128)(2,1)S(1)} %pad_maximum_fusion), channel_id=1, source_target_pairs={{0,8},{8,16},{16,24},{24,32},{32,40},{40,48},{48,56},{56,64},{64,7... | collective-permute-start | bytes 1179656 | tf_op jit(solution)/shard_map/ppermute | solution.py:21
  28.4 4.8 %collective-permute-done.1 = bf16[2,256,384]{1,2,0:T(8,128)(2,1)S(1)} collective-permute-done((bf16[2,256,384]{1,2,0:T(8,128)(2,1)S(1)}, bf16[2,256,384]{1,2,0:T(8,128)(2,1)S(1)}, u32[]{:S(2)}, u32[]{:S(2)}) %collective-permute-start.1) | collective-permute-done | bytes 393248 | tf_op jit(solution)/shard_map/ppermute | solution.py:21
  33.2 5.1 %collective-permute-start.3 = (bf16[2,256,384]{1,2,0:T(8,128)(2,1)S(1)}, bf16[2,256,384]{1,2,0:T(8,128)(2,1)S(1)}, u32[]{:S(2)}, u32[]{:S(2)}) collective-permute-start(bf16[2,256,384]{1,2,0:T(8,128)(2,1)S(1)} %collective-permute-done.1), channel_id=1, source_target_pairs={{0,8},{8,16},{16,24},{24,32},{32,40},{40,48},{48,56},{56,64},{64,7... | collective-permute-start | bytes 1179656 | tf_op jit(solution)/shard_map/ppermute | solution.py:21
  39.0 4.8 %collective-permute-done.3 = bf16[2,256,384]{1,2,0:T(8,128)(2,1)S(1)} collective-permute-done((bf16[2,256,384]{1,2,0:T(8,128)(2,1)S(1)}, bf16[2,256,384]{1,2,0:T(8,128)(2,1)S(1)}, u32[]{:S(2)}, u32[]{:S(2)}) %collective-permute-start.3) | collective-permute-done | bytes 393248 | tf_op jit(solution)/shard_map/ppermute | solution.py:21
  43.8 6.7 %collective-permute-start.5 = (bf16[2,256,384]{1,2,0:T(8,128)(2,1)S(1)}, bf16[2,256,384]{1,2,0:T(8,128)(2,1)S(1)}, u32[]{:S(2)}, u32[]{:S(2)}) collective-permute-start(bf16[2,256,384]{1,2,0:T(8,128)(2,1)S(1)} %collective-permute-done.3), channel_id=1, source_target_pairs={{0,8},{8,16},{16,24},{24,32},{32,40},{40,48},{48,56},{56,64},{64,7... | collective-permute-start | bytes 1179656 | tf_op jit(solution)/shard_map/ppermute | solution.py:21
  51.2 6.6 %collective-permute-done.5 = bf16[2,256,384]{1,2,0:T(8,128)(2,1)S(1)} collective-permute-done((bf16[2,256,384]{1,2,0:T(8,128)(2,1)S(1)}, bf16[2,256,384]{1,2,0:T(8,128)(2,1)S(1)}, u32[]{:S(2)}, u32[]{:S(2)}) %collective-permute-start.5) | collective-permute-done | bytes 393248 | tf_op jit(solution)/shard_map/ppermute | solution.py:21
  57.9 5.0 %collective-permute-start.7 = (bf16[2,256,384]{1,2,0:T(8,128)(2,1)S(1)}, bf16[2,256,384]{1,2,0:T(8,128)(2,1)S(1)}, u32[]{:S(2)}, u32[]{:S(2)}) collective-permute-start(bf16[2,256,384]{1,2,0:T(8,128)(2,1)S(1)} %collective-permute-done.5), channel_id=1, source_target_pairs={{0,8},{8,16},{16,24},{24,32},{32,40},{40,48},{48,56},{56,64},{64,7... | collective-permute-start | bytes 1179656 | tf_op jit(solution)/shard_map/ppermute | solution.py:21
  63.6 4.5 %collective-permute-done.7 = bf16[2,256,384]{1,2,0:T(8,128)(2,1)S(1)} collective-permute-done((bf16[2,256,384]{1,2,0:T(8,128)(2,1)S(1)}, bf16[2,256,384]{1,2,0:T(8,128)(2,1)S(1)}, u32[]{:S(2)}, u32[]{:S(2)}) %collective-permute-start.7) | collective-permute-done | bytes 393248 | tf_op jit(solution)/shard_map/ppermute | solution.py:21
  70.8 1.1 multiply_reduce_fusion.1
  71.8 10.0 %psum.21 = f32[256]{0:T(256)S(1)} all-reduce(f32[256]{0:T(256)S(1)} %get-tuple-element.48), channel_id=1, replica_groups=mesh['tm'=64,'head'=8] {'head'}, use_global_device_ids=true, to_apply=%region_11.12 | all-reduce | flops 256 | bytes 2048 | tf_op jit(solution)/shard_map/psum | solution.py:168
  81.8 2.0 copy.105
  83.8 1.7 fusion.47
  85.5 12.0 %psum.22 = f32[256]{0:T(256)} all-reduce(f32[256]{0:T(256)} %get-tuple-element.16), channel_id=1, replica_groups=mesh['tm'=64,'head'=8] {'head'}, use_global_device_ids=true, to_apply=%region_13.14 | all-reduce | flops 256 | bytes 2048 | tf_op jit(solution)/shard_map/psum | solution.py:168
  98.3 1.9 fusion.45
  100.2 1.1 copy.108
  101.2 1.1 multiply_reduce_fusion
  102.3 1.0 convolution_convert_fusion.3
  103.4 1.1 fusion.11
  104.5 1.1 fusion.12
  121.3 1.3 collective-permute-start.8
  123.4 1.3 collective-permute-start.9
  125.5 1.4 collective-permute-start.11
  127.7 1.3 collective-permute-start.10
  131.4 217.4 %psum.23 = f32[384]{0:T(512)} all-reduce(f32[384]{0:T(512)S(1)} %copy-done.40), channel_id=1, replica_groups=mesh['tm'=64,'head'=8] {'tm'}, use_global_device_ids=true, to_apply=%region_16.17 | all-reduce | flops 384 | bytes 3072 | tf_op jit(solution)/shard_map/psum | solution.py:176
  348.8 1.2 add_convert_fusion
  (148 shorter events, 28.2 us)
Async XLA Ops:
  1.4 15.9 %copy-start.37 = (bf16[256,384]{1,0:T(8,128)(2,1)S(1)}, bf16[256,384]{1,0:T(8,128)(2,1)}, u32[]{:S(2)}) copy-start(bf16[256,384]{1,0:T(8,128)(2,1)} %param.8) | copy-start | bytes 589828
  1.4 5.2 %collective-permute-start = (s32[256]{0:T(256)S(1)}, s32[256]{0:T(256)S(1)}, u32[]{:S(2)}, u32[]{:S(2)}) collective-permute-start(s32[256]{0:T(256)S(1)} %broadcast_bitcast_fusion), channel_id=1, source_target_pairs={{0,8},{8,16},{16,24},{24,32},{32,40},{40,48},{48,56},{56,64},{64,7... | collective-permute-start | bytes 3080 | tf_op jit(solution)/shard_map/ppermute | solution.py:21
  6.6 5.5 %collective-permute-start.2 = (s32[256]{0:T(256)S(1)}, s32[256]{0:T(256)S(1)}, u32[]{:S(2)}, u32[]{:S(2)}) collective-permute-start(s32[256]{0:T(256)S(1)} %collective-permute-done), channel_id=1, source_target_pairs={{0,8},{8,16},{16,24},{24,32},{32,40},{40,48},{48,56},{56,64},{64,7... | collective-permute-start | bytes 3080 | tf_op jit(solution)/shard_map/ppermute | solution.py:21
  12.0 5.5 %collective-permute-start.4 = (s32[256]{0:T(256)S(1)}, s32[256]{0:T(256)S(1)}, u32[]{:S(2)}, u32[]{:S(2)}) collective-permute-start(s32[256]{0:T(256)S(1)} %collective-permute-done.2), channel_id=1, source_target_pairs={{0,8},{8,16},{16,24},{24,32},{32,40},{40,48},{48,56},{56,64},{64,7... | collective-permute-start | bytes 3080 | tf_op jit(solution)/shard_map/ppermute | solution.py:21
  17.3 10.6 %copy-start.4 = (bf16[256,384]{0,1:T(8,128)(2,1)}, bf16[256,384]{0,1:T(8,128)(2,1)S(1)}, u32[]{:S(2)}) copy-start(bf16[256,384]{0,1:T(8,128)(2,1)S(1)} %copy.85) | copy-start | bytes 589828
  17.5 52.0 %copy-start.6 = (bf16[256,384]{0,1:T(8,128)(2,1)}, bf16[256,384]{0,1:T(8,128)(2,1)S(1)}, u32[]{:S(2)}) copy-start(bf16[256,384]{0,1:T(8,128)(2,1)S(1)} %copy.90) | copy-start | bytes 589828
  17.5 10.1 %collective-permute-start.6 = (s32[256]{0:T(256)S(1)}, s32[256]{0:T(256)S(1)}, u32[]{:S(2)}, u32[]{:S(2)}) collective-permute-start(s32[256]{0:T(256)S(1)} %collective-permute-done.4), channel_id=1, source_target_pairs={{0,8},{8,16},{16,24},{24,32},{32,40},{40,48},{48,56},{56,64},{64,7... | collective-permute-start | bytes 3080 | tf_op jit(solution)/shard_map/ppermute | solution.py:21
  21.8 5.6 %copy-start.38 = (bf16[256,384]{1,0:T(8,128)(2,1)S(1)}, bf16[256,384]{1,0:T(8,128)(2,1)}, u32[]{:S(2)}) copy-start(bf16[256,384]{1,0:T(8,128)(2,1)} %param.6) | copy-start | bytes 589828
  21.9 11.3 %collective-permute-start.1 = (bf16[2,256,384]{1,2,0:T(8,128)(2,1)S(1)}, bf16[2,256,384]{1,2,0:T(8,128)(2,1)S(1)}, u32[]{:S(2)}, u32[]{:S(2)}) collective-permute-start(bf16[2,256,384]{1,2,0:T(8,128)(2,1)S(1)} %pad_maximum_fusion), channel_id=1, source_target_pairs={{0,8},{8,16},{16,24},{24,32},{32,40},{40,48},{48,56},{56,64},{64,7... | collective-permute-start | bytes 1179656 | tf_op jit(solution)/shard_map/ppermute | solution.py:21
  27.9 41.9 %copy-start.14 = (pred[256,256]{0,1:T(8,128)(4,1)}, pred[256,256]{0,1:T(8,128)(4,1)S(1)}, u32[]{:S(2)}) copy-start(pred[256,256]{0,1:T(8,128)(4,1)S(1)} %get-tuple-element.33) | copy-start | bytes 196612
  27.9 42.2 %copy-start.12 = (pred[256,256]{0,1:T(8,128)(4,1)}, pred[256,256]{0,1:T(8,128)(4,1)S(1)}, u32[]{:S(2)}) copy-start(pred[256,256]{0,1:T(8,128)(4,1)S(1)} %get-tuple-element.34) | copy-start | bytes 196612
  27.9 42.5 %copy-start.10 = (pred[256,256]{0,1:T(8,128)(4,1)}, pred[256,256]{0,1:T(8,128)(4,1)S(1)}, u32[]{:S(2)}) copy-start(pred[256,256]{0,1:T(8,128)(4,1)S(1)} %get-tuple-element.35) | copy-start | bytes 196612
  27.9 42.9 %copy-start.8 = (pred[256,256]{0,1:T(8,128)(4,1)}, pred[256,256]{0,1:T(8,128)(4,1)S(1)}, u32[]{:S(2)}) copy-start(pred[256,256]{0,1:T(8,128)(4,1)S(1)} %get-tuple-element.36) | copy-start | bytes 196612
  33.2 10.6 %collective-permute-start.3 = (bf16[2,256,384]{1,2,0:T(8,128)(2,1)S(1)}, bf16[2,256,384]{1,2,0:T(8,128)(2,1)S(1)}, u32[]{:S(2)}, u32[]{:S(2)}) collective-permute-start(bf16[2,256,384]{1,2,0:T(8,128)(2,1)S(1)} %collective-permute-done.1), channel_id=1, source_target_pairs={{0,8},{8,16},{16,24},{24,32},{32,40},{40,48},{48,56},{56,64},{64,7... | collective-permute-start | bytes 1179656 | tf_op jit(solution)/shard_map/ppermute | solution.py:21
  38.4 31.4 %copy-start.18 = (bf16[1,256,384]{1,2,0:T(8,128)(2,1)}, bf16[1,256,384]{1,2,0:T(8,128)(2,1)S(1)}, u32[]{:S(2)}) copy-start(bf16[1,256,384]{1,2,0:T(8,128)(2,1)S(1)} %get-tuple-element.31) | copy-start | bytes 589828
  43.8 14.0 %collective-permute-start.5 = (bf16[2,256,384]{1,2,0:T(8,128)(2,1)S(1)}, bf16[2,256,384]{1,2,0:T(8,128)(2,1)S(1)}, u32[]{:S(2)}, u32[]{:S(2)}) collective-permute-start(bf16[2,256,384]{1,2,0:T(8,128)(2,1)S(1)} %collective-permute-done.3), channel_id=1, source_target_pairs={{0,8},{8,16},{16,24},{24,32},{32,40},{40,48},{48,56},{56,64},{64,7... | collective-permute-start | bytes 1179656 | tf_op jit(solution)/shard_map/ppermute | solution.py:21
  50.6 19.5 %copy-start.20 = (bf16[1,256,384]{1,2,0:T(8,128)(2,1)}, bf16[1,256,384]{1,2,0:T(8,128)(2,1)S(1)}, u32[]{:S(2)}) copy-start(bf16[1,256,384]{1,2,0:T(8,128)(2,1)S(1)} %get-tuple-element.29) | copy-start | bytes 589828
  57.9 10.3 %collective-permute-start.7 = (bf16[2,256,384]{1,2,0:T(8,128)(2,1)S(1)}, bf16[2,256,384]{1,2,0:T(8,128)(2,1)S(1)}, u32[]{:S(2)}, u32[]{:S(2)}) collective-permute-start(bf16[2,256,384]{1,2,0:T(8,128)(2,1)S(1)} %collective-permute-done.5), channel_id=1, source_target_pairs={{0,8},{8,16},{16,24},{24,32},{32,40},{40,48},{48,56},{56,64},{64,7... | collective-permute-start | bytes 1179656 | tf_op jit(solution)/shard_map/ppermute | solution.py:21
  62.9 7.5 %copy-start.22 = (bf16[1,256,384]{1,2,0:T(8,128)(2,1)}, bf16[1,256,384]{1,2,0:T(8,128)(2,1)S(1)}, u32[]{:S(2)}) copy-start(bf16[1,256,384]{1,2,0:T(8,128)(2,1)S(1)} %get-tuple-element.27) | copy-start | bytes 589828
  68.1 2.6 copy-start.24
  68.8 2.0 copy-start
  81.8 2.0 copy-start.36
  81.8 2.0 copy-start.39
  103.4 1.1 copy-start.21
  107.0 1.1 copy-start.1
  107.0 1.1 copy-start.9
  107.0 1.2 copy-start.25
  121.3 227.5 %collective-permute-start.8 = (bf16[2,256,384]{2,1,0:T(8,128)(2,1)}, bf16[2,256,384]{2,1,0:T(8,128)(2,1)S(1)}, u32[]{:S(2)}, u32[]{:S(2)}) collective-permute-start(bf16[2,256,384]{2,1,0:T(8,128)(2,1)} %pad_maximum_fusion.2), channel_id=1, source_target_pairs={{8,0},{16,8},{24,16},{32,24},{40,32},{48,40},{56,48},{64,56},{72,6... | collective-permute-start | bytes 1179656 | tf_op jit(solution)/shard_map/ppermute | solution.py:21
  123.4 225.4 %collective-permute-start.9 = (bf16[2,256,384]{2,1,0:T(8,128)(2,1)}, bf16[2,256,384]{2,1,0:T(8,128)(2,1)S(1)}, u32[]{:S(2)}, u32[]{:S(2)}) collective-permute-start(bf16[2,256,384]{2,1,0:T(8,128)(2,1)} %pad_maximum_fusion.3), channel_id=1, source_target_pairs={{16,0},{24,8},{32,16},{40,24},{48,32},{56,40},{64,48},{72,56},{80,... | collective-permute-start | bytes 1179656 | tf_op jit(solution)/shard_map/ppermute | solution.py:21
  125.5 3.5 %copy-start.17 = (bf16[1,256,384]{1,2,0:T(8,128)(2,1)S(1)}, bf16[1,256,384]{1,2,0:T(8,128)(2,1)}, u32[]{:S(2)}) copy-start(bf16[1,256,384]{1,2,0:T(8,128)(2,1)} %copy-done.16) | copy-start | bytes 589828
  125.5 223.3 %collective-permute-start.11 = (bf16[2,256,384]{2,1,0:T(8,128)(2,1)}, bf16[2,256,384]{2,1,0:T(8,128)(2,1)S(1)}, u32[]{:S(2)}, u32[]{:S(2)}) collective-permute-start(bf16[2,256,384]{2,1,0:T(8,128)(2,1)} %pad_maximum_fusion.5), channel_id=1, source_target_pairs={{32,0},{40,8},{48,16},{56,24},{64,32},{72,40},{80,48},{88,56},{96,... | collective-permute-start | bytes 1179656 | tf_op jit(solution)/shard_map/ppermute | solution.py:21
  127.7 221.1 %collective-permute-start.10 = (bf16[2,256,384]{2,1,0:T(8,128)(2,1)}, bf16[2,256,384]{2,1,0:T(8,128)(2,1)}, u32[]{:S(2)}, u32[]{:S(2)}) collective-permute-start(bf16[2,256,384]{2,1,0:T(8,128)(2,1)} %pad_maximum_fusion.4), channel_id=1, source_target_pairs={{24,0},{32,8},{40,16},{48,24},{56,32},{64,40},{72,48},{80,56},{88,... | collective-permute-start | bytes 1179656 | tf_op jit(solution)/shard_map/ppermute | solution.py:21
  (21 other events, 19.1 us)
where the time goes:
time: 352 us; the launch traced here: 351 us
  blocking collectives  239 us (68%)
  starting transfers between devices  44.2 us (13%)
  waiting for transfers between devices  23.4 us (7%)
  local copies, waits for them, and re-layouts  16.8 us (5%)
  matrix products  14 us (4%)
  other arithmetic  11.7 us (3%)
    psum x1, blocking collectives, body(): lax.psum(jnp.sum(grad_rows * flat_att * rms_inv[:, None], axis=0), 'tm')  217 us
    ppermute x12, starting transfers between devices, passed_along(): return lax.ppermute(x, axis, pairs)  44.2 us
    ppermute x12, waiting for transfers between devices, passed_along(): return lax.ppermute(x, axis, pairs)  23.4 us
    psum x2, blocking collectives, body(): lax.psum((jnp.sum(flat_att * flat_att, axis=1), jnp.sum(scaled * flat_att...  22 us
    unnamed x86, local copies, waits for them, and re-layouts  11.2 us
  transfers between devices with their start and end apart: 12, of which 6 were waited for; matrix products, arithmetic and copies ran while one was open for 2% of the time, Pallas kernels for 0%

commit v1 on v0

v1 whole, which is shorter than its diff:
```python
import functools

import jax
import jax.numpy as jnp
from jax import lax
from jax.experimental import pallas as pl
from jax.experimental.pallas import tpu as pltpu
from jax.sharding import PartitionSpec as P

HSZ = 128
BLK = 128
REACH = 4
NEG = -1e30
MESH = pl.DeviceIdType.MESH
F32 = jnp.float32
BF16 = jnp.bfloat16


def nt(a, b):
    return lax.dot_general(a, b, (((1,), (1,)), ((), ())), preferred_element_type=F32)


def tn(a, b):
    return lax.dot_general(a, b, (((0,), (0,)), ((), ())), preferred_element_type=F32)


def nn(a, b):
    return lax.dot_general(a, b, (((1,), (0,)), ((), ())), preferred_element_type=F32)


def radices(count):
    found, stride = [], 1
    while stride < count:
        radix = min(4, count // stride)
        found.append((stride, radix))
        stride *= radix
    return found


def kernel(
    n_tm,
    n_head,
    heads,
    stages,
    q_hbm,
    k_hbm,
    v_hbm,
    g_hbm,
    gain_ref,
    ids_ref,
    normed_ref,
    dq_ref,
    dk_ref,
    dv_ref,
    dgain_ref,
    qb,
    kb,
    vb,
    db,
    q4,
    k4,
    v4,
    d4,
    gb,
    ids_own,
    ids_prev,
    ids_next,
    stats_own,
    stats_next,
    s_ref,
    s4_ref,
    r_ref,
    r4_ref,
    out_acc,
    att_ref,
    sums_own,
    sums_in,
    gain_own,
    gain_in,
    dq_acc,
    dk_acc,
    dv_acc,
    local_sem,
    k_send,
    k_recv,
    q_send,
    q_recv,
    v_send,
    v_recv,
    d_send,
    d_recv,
    ip_send,
    ip_recv,
    in_send,
    in_recv,
    st_send,
    st_recv,
    hd_send,
    hd_recv,
    gn_send,
    gn_recv,
):
    tm = lax.axis_index("tm")
    head = lax.axis_index("head")
    later = (lax.rem(tm + 1, n_tm), head)
    earlier = (lax.rem(tm + n_tm - 1, n_tm), head)
    factor = HSZ ** (-0.5)
    features = HSZ * heads * n_head

    def local(which, src, dst, h):
        return pltpu.make_async_copy(
            src.at[:, h * HSZ : (h + 1) * HSZ], dst.at[h], local_sem.at[which, h]
        )

    loads = []
    for which, (src, dst) in enumerate(
        [(k_hbm, kb.at[0]), (q_hbm, qb.at[0]), (v_hbm, vb.at[0]), (g_hbm, gb)]
    ):
        loads.append([local(which, src, dst, h) for h in range(heads)])
        for one in loads[-1]:
            one.start()

    ids_own[...] = jnp.zeros(ids_own.shape, jnp.int32)
    ids_own[0:1, :] = jnp.full((1, BLK), ids_ref[0], jnp.int32)
    ids_own[1:2, :] = jnp.full((1, BLK), ids_ref[1], jnp.int32)

    def gain_peer(stage, off):
        stride, radix = stages[stage]
        digit = lax.rem(tm // stride, radix)
        return (tm + (lax.rem(digit + off, radix) - digit) * stride, head)

    barrier = pltpu.get_barrier_semaphore()
    greeted = [later, earlier]
    greeted += [(tm, lax.rem(head + off, n_head)) for off in range(1, n_head)]
    for stage, (_, radix) in enumerate(stages):
        greeted += [gain_peer(stage, off) for off in range(1, radix)]
    for peer in greeted:
        pl.semaphore_signal(barrier, inc=1, device_id=peer, device_id_type=MESH)
    pl.semaphore_wait(barrier, len(greeted))

    def remote(src, dst, send, recv, peer):
        return pltpu.make_async_remote_copy(
            src_ref=src,
            dst_ref=dst,
            send_sem=send,
            recv_sem=recv,
            device_id=peer,
            device_id_type=MESH,
        )

    def chain(full, last, send, recv, peer, rows, hop, h):
        if hop < REACH - 1:
            src, dst = full.at[hop, h], full.at[hop + 1, h]
        else:
            src, dst = full.at[hop, h, rows, :], last.at[h]
        return remote(src, dst, send.at[hop, h], recv.at[hop, h], peer)

    low, high = pl.ds(0, BLK), pl.ds(BLK, BLK)
    k_hop = functools.partial(chain, kb, k4, k_send, k_recv, later, high)
    v_hop = functools.partial(chain, vb, v4, v_send, v_recv, later, high)
    q_hop = functools.partial(chain, qb, q4, q_send, q_recv, earlier, low)
    d_hop = functools.partial(chain, db, d4, d_send, d_recv, earlier, low)

    def small_hop(own, got, send, recv, peer, hop):
        src = own if hop == 0 else got.at[hop - 1]
        return remote(src, got.at[hop], send.at[hop], recv.at[hop], peer)

    ip_hop = functools.partial(small_hop, ids_own, ids_prev, ip_send, ip_recv, later)
    in_hop = functools.partial(small_hop, ids_own, ids_next, in_send, in_recv, earlier)
    st_hop = functools.partial(small_hop, stats_own, stats_next, st_send, st_recv, earlier)

    def over_heads(step):
        lax.fori_loop(0, heads, lambda h, c: (step(h), c)[1], 0)

    def bias_row(key_row, query_rows):
        parts = [jnp.where(key_row == row, 0.0, NEG).astype(F32) for row in query_rows]
        return parts[0] if len(parts) == 1 else jnp.concatenate(parts, axis=1)

    ip_hop(0).start()
    in_hop(0).start()
    for h in range(heads):
        loads[0][h].wait()
        k_hop(0, h).start()
        loads[1][h].wait()
        q_hop(0, h).start()

    own_rows = [ids_own[0:1, :], ids_own[1:2, :]]

    def score_block(dst, keys, queries, biases):
        for part in range(2):
            rows = pl.ds(part * BLK, BLK)
            dst[rows, :] = nt(keys[rows, :], queries[...]) * factor + biases[part]

    own_bias = [bias_row(own_rows[p], own_rows) for p in range(2)]
    over_heads(lambda h: score_block(s_ref.at[0, h], kb.at[0, h], qb.at[0, h], own_bias))

    for d in range(1, REACH):
        ip_hop(d - 1).wait_recv()
        ip_hop(d).start()
        in_hop(d - 1).wait_recv()
        in_hop(d).start()
        prev_rows = [ids_prev[d - 1, 0:1, :], ids_prev[d - 1, 1:2, :]]
        next_rows = [ids_next[d - 1, 0:1, :], ids_next[d - 1, 1:2, :]]
        s_bias = [bias_row(prev_rows[p], own_rows) for p in range(2)]
        r_bias = [bias_row(own_rows[p], next_rows) for p in range(2)]

        def arrive(h, d=d, s_bias=s_bias, r_bias=r_bias):
            k_hop(d - 1, h).wait_recv()
            k_hop(d, h).start()
            q_hop(d - 1, h).wait_recv()
            q_hop(d, h).start()
            score_block(s_ref.at[d, h], kb.at[d, h], qb.at[0, h], s_bias)
            score_block(r_ref.at[d - 1, h], kb.at[0, h], qb.at[d, h], r_bias)

        over_heads(arrive)

    for h in range(heads):
        loads[2][h].wait()
        v_hop(0, h).start()
    ip_hop(3).wait_recv()
    in_hop(3).wait_recv()
    s4_bias = bias_row(ids_prev[3, 1:2, :], [own_rows[0]])
    r4_bias = bias_row(own_rows[1], [ids_next[3, 0:1, :]])

    def soften(h):
        k_hop(3, h).wait_recv()
        q_hop(3, h).wait_recv()
        s4 = nt(k4[h], qb[0, h, 0:BLK, :]) * factor + s4_bias
        r4_ref[h] = nt(kb[0, h, BLK : 2 * BLK, :], q4[h]) * factor + r4_bias
        top = jnp.max(s_ref[0, h], axis=0, keepdims=True)
        for d in range(1, REACH):
            top = jnp.maximum(top, jnp.max(s_ref[d, h], axis=0, keepdims=True))
        top4 = jnp.max(s4, axis=0, keepdims=True)
        top_low = jnp.maximum(top[:, 0:BLK], top4)
        top = jnp.concatenate([top_low, top[:, BLK:]], axis=1)
        e4 = jnp.exp(s4 - top_low)
        total4 = jnp.sum(e4, axis=0, keepdims=True)
        total = jnp.concatenate([total4, jnp.zeros((1, BLK), F32)], axis=1)
        for d in range(REACH):
            e = jnp.exp(s_ref[d, h] - top)
            s_ref[d, h] = e
            total = total + jnp.sum(e, axis=0, keepdims=True)
        inverse = 1.0 / total
        for d in range(REACH):
            s_ref[d, h] = s_ref[d, h] * inverse
        s4_ref[h] = e4 * inverse[:, 0:BLK]
        stats_own[pl.ds(h, 1), :] = top + jnp.log(total)
        out_acc[h] = tn(s_ref[0, h].astype(BF16), vb[0, h])

    stats_own[...] = jnp.zeros(stats_own.shape, F32)
    over_heads(soften)

    for d in range(1, REACH):

        def attend(h, d=d):
            v_hop(d - 1, h).wait_recv()
            v_hop(d, h).start()
            out_acc[h] += tn(s_ref[d, h].astype(BF16), vb[d, h])

        over_heads(attend)

    for h in range(heads):
        loads[3][h].wait()
    square = jnp.zeros((2 * BLK, HSZ), F32)
    cross = jnp.zeros((2 * BLK, HSZ), F32)
    for h in range(heads):
        v_hop(3, h).wait_recv()
        out_acc[h, 0:BLK, :] += tn(s4_ref[h].astype(BF16), v4[h])
        att_b = out_acc[h].astype(BF16)
        att_ref[h] = att_b
        att = att_b.astype(F32)
        scaled = gb[h].astype(F32) * gain_ref[:, h * HSZ : (h + 1) * HSZ]
        square = square + att * att
        cross = cross + scaled * att
    sums_own[...] = jnp.zeros(sums_own.shape, F32)
    sums_own[0:1, :] = jnp.sum(square.T, axis=0, keepdims=True)
    sums_own[1:2, :] = jnp.sum(cross.T, axis=0, keepdims=True)

    def head_copy(off):
        return remote(
            sums_own,
            sums_in.at[off - 1],
            hd_send.at[off - 1],
            hd_recv.at[off - 1],
            (tm, lax.rem(head + off, n_head)),
        )

    for off in range(1, n_head):
        head_copy(off).start()
    sums = sums_own[...]
    for off in range(1, n_head):
        head_copy(off).wait_recv()
        sums = sums + sums_in[off - 1]
    rms_row = 1.0 / jnp.sqrt(sums[0:1, :] / features + 1e-06)
    pull_row = rms_row * rms_row * sums[1:2, :] / features
    rms = jnp.broadcast_to(rms_row, (HSZ, 2 * BLK)).T
    pull = jnp.broadcast_to(pull_row, (HSZ, 2 * BLK)).T

    gain_own[...] = jnp.zeros(gain_own.shape, F32)
    for h in range(heads):
        cols = slice(h * HSZ, (h + 1) * HSZ)
        att = att_ref[h].astype(F32)
        grad = gb[h].astype(F32)
        gain = gain_ref[:, cols]
        grad_att = (rms * (grad * gain - att * pull)).astype(BF16)
        db[0, h] = grad_att
        delta = att * grad_att.astype(F32)
        stats_own[heads + h : heads + h + 1, :] = jnp.sum(delta.T, axis=0, keepdims=True)
        d_hop(0, h).start()
        scaled_att = att * rms
        normed_ref[:, cols] = (scaled_att * gain).astype(BF16)
        gain_own[0, h : h + 1, :] = jnp.sum(grad * scaled_att, axis=0, keepdims=True)
    st_hop(0).start()

    def gain_copy(stage, off):
        return remote(
            gain_own.at[stage],
            gain_in.at[stage, off - 1],
            gn_send.at[stage, off - 1],
            gn_recv.at[stage, off - 1],
            gain_peer(stage, off),
        )

    def gain_begin(stage):
        for off in range(1, stages[stage][1]):
            gain_copy(stage, off).start()

    def gain_end(stage):
        total = gain_own[stage]
        for off in range(1, stages[stage][1]):
            gain_copy(stage, off).wait_recv()
            total = total + gain_in[stage, off - 1]
        gain_own[stage + 1] = total

    gain_begin(0)

    def own_block(h):
        weights = s_ref[0, h]
        grad_h = db[0, h]
        delta = stats_own[pl.ds(heads + h, 1), :]
        dscore = (weights * (nt(vb[0, h], grad_h) - delta)).astype(BF16)
        dq_acc[h] = tn(dscore, kb[0, h])
        dk_acc[h] = nn(dscore, qb[0, h])
        dv_acc[h] = nn(weights.astype(BF16), grad_h)

    over_heads(own_block)

    for d in range(1, REACH):
        st_hop(d - 1).wait_recv()
        st_hop(d).start()

        def backward(h, d=d):
            d_hop(d - 1, h).wait_recv()
            d_hop(d, h).start()
            delta = stats_own[pl.ds(heads + h, 1), :]
            dscore = (s_ref[d, h] * (nt(vb[d, h], db[0, h]) - delta)).astype(BF16)
            dq_acc[h] += tn(dscore, kb[d, h])
            log_total = stats_next[d - 1, pl.ds(h, 1), :]
            delta = stats_next[d - 1, pl.ds(heads + h, 1), :]
            weights = jnp.exp(r_ref[d - 1, h] - log_total)
            grad_h = db[d, h]
            dv_acc[h] += nn(weights.astype(BF16), grad_h)
            dscore = (weights * (nt(vb[0, h], grad_h) - delta)).astype(BF16)
            dk_acc[h] += nn(dscore, qb[d, h])

        over_heads(backward)
        if d - 1 < len(stages):
            gain_end(d - 1)
            if d < len(stages):
                gain_begin(d)

    st_hop(3).wait_recv()
    for h in range(heads):
        cols = slice(h * HSZ, (h + 1) * HSZ)
        delta = stats_own[heads + h : heads + h + 1, 0:BLK]
        dscore = (s4_ref[h] * (nt(v4[h], db[0, h, 0:BLK, :]) - delta)).astype(BF16)
        dq_acc[h, 0:BLK, :] += tn(dscore, k4[h])
        dq_ref[:, cols] = (dq_acc[h] * factor).astype(BF16)
    for h in range(heads):
        cols = slice(h * HSZ, (h + 1) * HSZ)
        d_hop(3, h).wait_recv()
        log_total = stats_next[3, h : h + 1, 0:BLK]
        delta = stats_next[3, heads + h : heads + h + 1, 0:BLK]
        weights = jnp.exp(r4_ref[h] - log_total)
        grad_h = d4[h]
        dv_acc[h, BLK : 2 * BLK, :] += nn(weights.astype(BF16), grad_h)
        dscore = (weights * (nt(vb[0, h, BLK : 2 * BLK, :], grad_h) - delta)).astype(BF16)
        dk_acc[h, BLK : 2 * BLK, :] += nn(dscore, q4[h])
        dk_ref[:, cols] = (dk_acc[h] * factor).astype(BF16)
        dv_ref[:, cols] = dv_acc[h].astype(BF16)
        dgain_ref[0:1, cols] = gain_own[len(stages), h : h + 1, :]

    for hop in range(REACH):
        ip_hop(hop).wait_send()
        in_hop(hop).wait_send()
        st_hop(hop).wait_send()
        for h in range(heads):
            k_hop(hop, h).wait_send()
            q_hop(hop, h).wait_send()
            v_hop(hop, h).wait_send()
            d_hop(hop, h).wait_send()
    for off in range(1, n_head):
        head_copy(off).wait_send()
    for stage, (_, radix) in enumerate(stages):
        for off in range(1, radix):
            gain_copy(stage, off).wait_send()


def body(queries, key_rows, value_rows, grad_normed, norm_gain, utter_ids):
    rows, width = queries.shape
    heads = width // HSZ
    n_tm, n_head = lax.axis_size("tm"), lax.axis_size("head")
    stages = radices(n_tm)
    full = pltpu.VMEM((REACH, heads, rows, HSZ), BF16)
    last = pltpu.VMEM((heads, BLK, HSZ), BF16)
    wide = pltpu.VMEM((heads, rows, HSZ), F32)
    dma = pltpu.SemaphoreType.DMA
    hops = [dma((REACH, heads))] * 8 + [dma((REACH,))] * 6
    most = max(radix for _, radix in stages) - 1
    scratch = [full] * 4 + [last] * 4
    scratch += [
        pltpu.VMEM((heads, rows, HSZ), BF16),
        pltpu.VMEM((8, BLK), jnp.int32),
        pltpu.VMEM((REACH, 8, BLK), jnp.int32),
        pltpu.VMEM((REACH, 8, BLK), jnp.int32),
        pltpu.VMEM((8, rows), F32),
        pltpu.VMEM((REACH, 8, rows), F32),
        pltpu.VMEM((REACH, heads, rows, rows), F32),
        pltpu.VMEM((heads, BLK, BLK), F32),
        pltpu.VMEM((REACH - 1, heads, rows, rows), F32),
        pltpu.VMEM((heads, BLK, BLK), F32),
        wide,
        pltpu.VMEM((heads, rows, HSZ), BF16),
        pltpu.VMEM((8, rows), F32),
        pltpu.VMEM((n_head - 1, 8, rows), F32),
        pltpu.VMEM((len(stages) + 1, 8, HSZ), F32),
        pltpu.VMEM((len(stages), most, 8, HSZ), F32),
        wide,
        wide,
        wide,
        dma((4, heads)),
    ]
    scratch += hops
    scratch += [dma((n_head - 1,))] * 2 + [dma((len(stages), most))] * 2
    hbm = pl.BlockSpec(memory_space=pl.ANY)
    vmem = pl.BlockSpec(memory_space=pltpu.VMEM)
    big = jax.ShapeDtypeStruct((rows, width), BF16)
    outs = pl.pallas_call(
        functools.partial(kernel, n_tm, n_head, heads, stages),
        out_shape=[big] * 4 + [jax.ShapeDtypeStruct((1, width), F32)],
        in_specs=[hbm] * 4 + [vmem, pl.BlockSpec(memory_space=pltpu.SMEM)],
        out_specs=[vmem] * 5,
        scratch_shapes=scratch,
        compiler_params=pltpu.CompilerParams(collective_id=0, has_side_effects=True),
        name="attention_step",
    )(queries, key_rows, value_rows, grad_normed, norm_gain.reshape(1, width), utter_ids)
    return (*outs[:4], outs[4].reshape(width))


def solution(mesh):
    in_specs = (
        P("tm", "head"),
        P("tm", "head"),
        P("tm", "head"),
        P("tm", "head"),
        P("head"),
        P("tm"),
    )
    out_specs = (P("tm", "head"), P("tm", "head"), P("tm", "head"), P("tm", "head"), P("head"))
    return jax.shard_map(body, mesh=mesh, in_specs=in_specs, out_specs=out_specs, check_vma=False)
```

time: 352 us -> 88.6 us (0.25)
  blocking collectives: 239 us -> 0 us
  Pallas kernels: 0 us -> 79.9 us
  starting transfers between devices: 44.2 us -> 0 us
  waiting for transfers between devices: 23.4 us -> 0 us
  matrix products: 14 us -> 0 us
  other arithmetic: 11.7 us -> 0.6 us
  local copies, waits for them, and re-layouts: 16.8 us -> 6.24 us
    psum x3 -> x0, blocking collectives: 239 us -> none  [the longest x1 217 us: body(): lax.psum(jnp.sum(grad_rows * flat_att * rms_inv[:, None], axis=0), 'tm')]
    pallas_call x0 -> x1, Pallas kernels: none -> 79.9 us  [body(): pl.pallas_call(functools.partial(kernel, n_tm, n_head, heads, stages), ou...]
    ppermute x12 -> x0, starting transfers between devices: 44.2 us -> none  [passed_along(): return lax.ppermute(x, axis, pairs)]
    ppermute x12 -> x0, waiting for transfers between devices: 23.4 us -> none  [passed_along(): return lax.ppermute(x, axis, pairs)]
    dot_general x30 -> x0, matrix products: 14 us -> none  [the longest x5 3.7 us: query_step(): jnp.einsum('hqk,qhe->khe', weights_b, grad_heads, preferred_element_type=...]
    unnamed x86 -> x12, local copies, waits for them, and re-layouts: 11.2 us -> 4.99 us
    another operation x7 -> x0, other arithmetic: 4.56 us -> none  [the longest x5 3.28 us: body(): jnp.stack([key_grad.reshape(row_count, feat_width), value_grad.reshape(ro...]
    convert_element_type x3 -> x0, local copies, waits for them, and re-layouts: 3.79 us -> none  [the longest x1 1.95 us: body(): flat_att = attended.reshape(row_count, feat_width).astype(jnp.float32)]
  transfers between devices with their start and end apart: 12 -> 0, of which waited for: 6 -> 0; matrix products, arithmetic and copies ran while one was open for 2% -> 0% of each run, Pallas kernels for 0% -> 0%
where the time goes in v1:
time: 88.6 us; the launch traced here: 87.4 us
  Pallas kernels  79.9 us (90%)
  local copies, waits for them, and re-layouts  6.24 us (7%)
    pallas_call x1, Pallas kernels, body(): pl.pallas_call(functools.partial(kernel, n_tm, n_head, heads, stages), ou...  79.9 us
    unnamed x12, local copies, waits for them, and re-layouts  4.99 us

profile of v1, /device:TPU:6, one launch (start us, length us, event | category | flops | bytes accessed | tf_op | source)
XLA Modules:
  0.0 87.4 jit_solution(13398356788285794023)
XLA Ops:
  0.6 1.2 %reshape.16.gain_ref = f32[1,384]{1,0:T(1,128)} reshape(f32[384]{0:T(512)} %param.10) | data formatting | bytes 3072 | tf_op jit(solution)/shard_map/reshape | solution.py:456
  1.9 79.9 %attention_step.1 = (bf16[256,384]{1,0:T(8,128)(2,1)}, bf16[256,384]{1,0:T(8,128)(2,1)}, bf16[256,384]{1,0:T(8,128)(2,1)}, bf16[256,384]{1,0:T(8,128)(2,1)}, f32[1,384]{1,0:T(1,128)}) custom-call(bf16[256,384]{1,0:T(8,128)(2,1)} %q_hbm.1, bf16[256,384]{1,0:T(8,128)(2,1)} %k_hbm.1, bf16[256,384]{1,0:T(8,128)(2,1)} %v_hbm.1, bf16[256,384]{1,0:T(8,128)(2,1)} %g_hbm.1, ...), custom_call_target="tpu_custom_call" | custom-call | tf_op jit(solution)/shard_map/attention_step/pallas_call | solution.py:448
  81.8 0.0 copy-start.3
  81.8 0.7 copy-done.3
  82.5 0.6 reduce
  83.1 0.0 copy-start.2
  83.1 1.7 %copy.15 = bf16[256,384]{1,0:T(8,128)(2,1)} copy(bf16[256,384]{1,0:T(8,128)(2,1)} %get-tuple-element.20) | data formatting | bytes 393216
  84.8 0.0 copy-done.2
  84.8 0.0 copy-start.1
  84.8 0.7 copy.16
  85.4 0.3 copy-done.1
  85.8 0.0 copy-start
  85.8 0.7 copy.17
  86.4 0.3 copy-done
  86.8 0.7 copy.18
Async XLA Ops:
  81.8 0.7 copy-start.3
  83.1 1.7 %copy-start.2 = (bf16[256,384]{1,0:T(8,128)(2,1)S(1)}, bf16[256,384]{1,0:T(8,128)(2,1)}, u32[]{:S(2)}) copy-start(bf16[256,384]{1,0:T(8,128)(2,1)} %get-tuple-element.21) | copy-start | bytes 589828
  84.8 1.0 %copy-start.1 = (bf16[256,384]{1,0:T(8,128)(2,1)S(1)}, bf16[256,384]{1,0:T(8,128)(2,1)}, u32[]{:S(2)}) copy-start(bf16[256,384]{1,0:T(8,128)(2,1)} %get-tuple-element.22) | copy-start | bytes 589828
  85.8 1.0 %copy-start = (bf16[256,384]{1,0:T(8,128)(2,1)S(1)}, bf16[256,384]{1,0:T(8,128)(2,1)}, u32[]{:S(2)}) copy-start(bf16[256,384]{1,0:T(8,128)(2,1)} %get-tuple-element.23) | copy-start | bytes 589828

commit v2 on v1

--- a/solution.py
+++ b/solution.py
@@ -269,7 +269,7 @@
         att_b = out_acc[h].astype(BF16)
         att_ref[h] = att_b
         att = att_b.astype(F32)
-        scaled = gb[h].astype(F32) * gain_ref[:, h * HSZ : (h + 1) * HSZ]
+        scaled = gb[h].astype(F32) * gain_ref[h * HSZ : (h + 1) * HSZ].reshape(1, HSZ)
         square = square + att * att
         cross = cross + scaled * att
     sums_own[...] = jnp.zeros(sums_own.shape, F32)
@@ -301,7 +301,7 @@
         cols = slice(h * HSZ, (h + 1) * HSZ)
         att = att_ref[h].astype(F32)
         grad = gb[h].astype(F32)
-        gain = gain_ref[:, cols]
+        gain = gain_ref[cols].reshape(1, HSZ)
         grad_att = (rms * (grad * gain - att * pull)).astype(BF16)
         db[0, h] = grad_att
         delta = att * grad_att.astype(F32)
@@ -404,6 +404,18 @@
     for stage, (_, radix) in enumerate(stages):
         for off in range(1, radix):
             gain_copy(stage, off).wait_send()
+
+
+def put_out(*refs):
+    ins, outs, sem = refs[:5], refs[5:10], refs[10]
+    copies = [pltpu.make_async_copy(ins[i], outs[i], sem.at[i]) for i in range(4)]
+    for one in copies:
+        one.start()
+    for h in range(outs[4].shape[0] // HSZ):
+        cols = slice(h * HSZ, (h + 1) * HSZ)
+        outs[4][cols] = ins[4][0:1, cols].reshape(HSZ)
+    for one in copies:
+        one.wait()
 
 
 def body(queries, key_rows, value_rows, grad_normed, norm_gain, utter_ids):
@@ -453,8 +465,17 @@
         scratch_shapes=scratch,
         compiler_params=pltpu.CompilerParams(collective_id=0, has_side_effects=True),
         name="attention_step",
-    )(queries, key_rows, value_rows, grad_normed, norm_gain.reshape(1, width), utter_ids)
-    return (*outs[:4], outs[4].reshape(width))
+    )(queries, key_rows, value_rows, grad_normed, norm_gain, utter_ids)
+    return tuple(
+        pl.pallas_call(
+            put_out,
+            out_shape=[big] * 4 + [jax.ShapeDtypeStruct((width,), F32)],
+            in_specs=[vmem] * 5,
+            out_specs=[hbm] * 4 + [vmem],
+            scratch_shapes=[dma((4,))],
+            name="put_out",
+        )(*outs)
+    )
 
 
 def solution(mesh):

time: 88.6 us -> 84.4 us (0.953)
  local copies, waits for them, and re-layouts: 6.24 us -> 0 us
  Pallas kernels: 79.9 us -> 82.6 us
    unnamed x12 -> x0, local copies, waits for them, and re-layouts: 4.99 us -> none
    pallas_call x0 -> x1, Pallas kernels: none -> 2.69 us  [body(): pl.pallas_call(put_out, out_shape=[big] * 4 + [jax.ShapeDtypeStruct((widt...]
    reshape x1 -> x0, local copies, waits for them, and re-layouts: 1.25 us -> none  [body(): norm_gain.reshape(1, width)]
where the time goes in v2:
time: 84.4 us; the launch traced here: 83.3 us
  Pallas kernels  82.6 us (98%)
    pallas_call x1, Pallas kernels, body(): pl.pallas_call(functools.partial(kernel, n_tm, n_head, heads, stages), ou...  80 us
    pallas_call x1, Pallas kernels, body(): pl.pallas_call(put_out, out_shape=[big] * 4 + [jax.ShapeDtypeStruct((widt...  2.69 us

profile of v2, /device:TPU:6, one launch (start us, length us, event | category | flops | bytes accessed | tf_op | source)
XLA Modules:
  0.0 83.3 jit_solution(235058343697971828)
XLA Ops:
  0.6 80.0 %attention_step.1 = (bf16[256,384]{1,0:T(8,128)(2,1)}, bf16[256,384]{1,0:T(8,128)(2,1)}, bf16[256,384]{1,0:T(8,128)(2,1)}, bf16[256,384]{1,0:T(8,128)(2,1)}, f32[1,384]{1,0:T(1,128)}) custom-call(bf16[256,384]{1,0:T(8,128)(2,1)} %q_hbm.1, bf16[256,384]{1,0:T(8,128)(2,1)} %k_hbm.1, bf16[256,384]{1,0:T(8,128)(2,1)} %v_hbm.1, bf16[256,384]{1,0:T(8,128)(2,1)} %g_hbm.1, ...), custom_call_target="tpu_custom_call" | custom-call | tf_op jit(solution)/shard_map/attention_step/pallas_call | solution.py:460
  80.6 2.7 %put_out.1 = (bf16[256,384]{1,0:T(8,128)(2,1)}, bf16[256,384]{1,0:T(8,128)(2,1)}, bf16[256,384]{1,0:T(8,128)(2,1)}, bf16[256,384]{1,0:T(8,128)(2,1)}, f32[384]{0:T(512)}) custom-call(bf16[256,384]{1,0:T(8,128)(2,1)} %get-tuple-element.10.refs_0_, bf16[256,384]{1,0:T(8,128)(2,1)} %get-tuple-element.11.refs_1_, bf16[256,384]{1,0:T(8,128)(2,1)} %get-tuple-element.12.refs_2_, ...), custom_call_target="tpu_custom_call" | custom-call | tf_op jit(solution)/shard_map/put_out/pallas_call | solution.py:470

commit v3 on v2

--- a/solution.py
+++ b/solution.py
@@ -56,12 +56,14 @@
     qb,
     kb,
     vb,
-    db,
+    gb,
+    ab,
     q4,
     k4,
     v4,
-    d4,
-    gb,
+    g4,
+    a4,
+    db,
     ids_own,
     ids_prev,
     ids_next,
@@ -72,7 +74,6 @@
     r_ref,
     r4_ref,
     out_acc,
-    att_ref,
     sums_own,
     sums_in,
     gain_own,
@@ -80,6 +81,9 @@
     dq_acc,
     dk_acc,
     dv_acc,
+    gain_rows,
+    rms_d,
+    pull_d,
     local_sem,
     k_send,
     k_recv,
@@ -87,8 +91,10 @@
     q_recv,
     v_send,
     v_recv,
-    d_send,
-    d_recv,
+    g_send,
+    g_recv,
+    a_send,
+    a_recv,
     ip_send,
     ip_recv,
     in_send,
@@ -114,7 +120,7 @@
 
     loads = []
     for which, (src, dst) in enumerate(
-        [(k_hbm, kb.at[0]), (q_hbm, qb.at[0]), (v_hbm, vb.at[0]), (g_hbm, gb)]
+        [(k_hbm, kb.at[0]), (q_hbm, qb.at[0]), (v_hbm, vb.at[0]), (g_hbm, gb.at[0])]
     ):
         loads.append([local(which, src, dst, h) for h in range(heads)])
         for one in loads[-1]:
@@ -159,7 +165,8 @@
     k_hop = functools.partial(chain, kb, k4, k_send, k_recv, later, high)
     v_hop = functools.partial(chain, vb, v4, v_send, v_recv, later, high)
     q_hop = functools.partial(chain, qb, q4, q_send, q_recv, earlier, low)
-    d_hop = functools.partial(chain, db, d4, d_send, d_recv, earlier, low)
+    g_hop = functools.partial(chain, gb, g4, g_send, g_recv, earlier, low)
+    a_hop = functools.partial(chain, ab, a4, a_send, a_recv, earlier, low)
 
     def small_hop(own, got, send, recv, peer, hop):
         src = own if hop == 0 else got.at[hop - 1]
@@ -217,6 +224,8 @@
     for h in range(heads):
         loads[2][h].wait()
         v_hop(0, h).start()
+        loads[3][h].wait()
+        g_hop(0, h).start()
     ip_hop(3).wait_recv()
     in_hop(3).wait_recv()
     s4_bias = bias_row(ids_prev[3, 1:2, :], [own_rows[0]])
@@ -255,23 +264,24 @@
         def attend(h, d=d):
             v_hop(d - 1, h).wait_recv()
             v_hop(d, h).start()
+            g_hop(d - 1, h).wait_recv()
+            g_hop(d, h).start()
             out_acc[h] += tn(s_ref[d, h].astype(BF16), vb[d, h])
 
         over_heads(attend)
 
-    for h in range(heads):
-        loads[3][h].wait()
     square = jnp.zeros((2 * BLK, HSZ), F32)
     cross = jnp.zeros((2 * BLK, HSZ), F32)
     for h in range(heads):
         v_hop(3, h).wait_recv()
         out_acc[h, 0:BLK, :] += tn(s4_ref[h].astype(BF16), v4[h])
         att_b = out_acc[h].astype(BF16)
-        att_ref[h] = att_b
+        ab[0, h] = att_b
         att = att_b.astype(F32)
-        scaled = gb[h].astype(F32) * gain_ref[h * HSZ : (h + 1) * HSZ].reshape(1, HSZ)
+        scaled = gb[0, h].astype(F32) * gain_ref[h * HSZ : (h + 1) * HSZ].reshape(1, HSZ)
         square = square + att * att
         cross = cross + scaled * att
+        a_hop(0, h).start()
     sums_own[...] = jnp.zeros(sums_own.shape, F32)
     sums_own[0:1, :] = jnp.sum(square.T, axis=0, keepdims=True)
     sums_own[1:2, :] = jnp.sum(cross.T, axis=0, keepdims=True)
@@ -293,24 +303,35 @@
         sums = sums + sums_in[off - 1]
     rms_row = 1.0 / jnp.sqrt(sums[0:1, :] / features + 1e-06)
     pull_row = rms_row * rms_row * sums[1:2, :] / features
-    rms = jnp.broadcast_to(rms_row, (HSZ, 2 * BLK)).T
-    pull = jnp.broadcast_to(pull_row, (HSZ, 2 * BLK)).T
-
+    stats_own[2 * heads : 2 * heads + 1, :] = rms_row
+    stats_own[2 * heads + 1 : 2 * heads + 2, :] = pull_row
+
+    def column(row, count):
+        return jnp.broadcast_to(row, (HSZ, count)).T
+
+    def cotangent(att_b, grad_b, gain, rms, pull):
+        return (rms * (grad_b.astype(F32) * gain - att_b.astype(F32) * pull)).astype(BF16)
+
+    rms = column(rms_row, 2 * BLK)
+    pull = column(pull_row, 2 * BLK)
+    for h in range(heads):
+        gain = gain_ref[h * HSZ : (h + 1) * HSZ].reshape(1, HSZ)
+        att_b = ab[0, h]
+        grad_att = cotangent(att_b, gb[0, h], gain, rms, pull)
+        db[h] = grad_att
+        delta = att_b.astype(F32) * grad_att.astype(F32)
+        stats_own[heads + h : heads + h + 1, :] = jnp.sum(delta.T, axis=0, keepdims=True)
+    st_hop(0).start()
     gain_own[...] = jnp.zeros(gain_own.shape, F32)
     for h in range(heads):
+        a_hop(0, h).wait_recv()
+        a_hop(1, h).start()
         cols = slice(h * HSZ, (h + 1) * HSZ)
-        att = att_ref[h].astype(F32)
-        grad = gb[h].astype(F32)
-        gain = gain_ref[cols].reshape(1, HSZ)
-        grad_att = (rms * (grad * gain - att * pull)).astype(BF16)
-        db[0, h] = grad_att
-        delta = att * grad_att.astype(F32)
-        stats_own[heads + h : heads + h + 1, :] = jnp.sum(delta.T, axis=0, keepdims=True)
-        d_hop(0, h).start()
-        scaled_att = att * rms
-        normed_ref[:, cols] = (scaled_att * gain).astype(BF16)
-        gain_own[0, h : h + 1, :] = jnp.sum(grad * scaled_att, axis=0, keepdims=True)
-    st_hop(0).start()
+        scaled_att = ab[0, h].astype(F32) * rms
+        normed_ref[:, cols] = (scaled_att * gain_ref[cols].reshape(1, HSZ)).astype(BF16)
+        gain_own[0, h : h + 1, :] = jnp.sum(
+            gb[0, h].astype(F32) * scaled_att, axis=0, keepdims=True
+        )
 
     def gain_copy(stage, off):
         return remote(
@@ -335,8 +356,10 @@
     gain_begin(0)
 
     def own_block(h):
+        a_hop(1, h).wait_recv()
+        a_hop(2, h).start()
         weights = s_ref[0, h]
-        grad_h = db[0, h]
+        grad_h = db[h]
         delta = stats_own[pl.ds(heads + h, 1), :]
         dscore = (weights * (nt(vb[0, h], grad_h) - delta)).astype(BF16)
         dq_acc[h] = tn(dscore, kb[0, h])
@@ -345,20 +368,29 @@
 
     over_heads(own_block)
 
+    for h in range(heads):
+        cols = slice(h * HSZ, (h + 1) * HSZ)
+        gain_rows[h] = jnp.broadcast_to(gain_ref[cols].reshape(1, HSZ), (8, HSZ))
+
     for d in range(1, REACH):
         st_hop(d - 1).wait_recv()
         st_hop(d).start()
+        rms_d[...] = column(stats_next[d - 1, 2 * heads : 2 * heads + 1, :], 2 * BLK)
+        pull_d[...] = column(stats_next[d - 1, 2 * heads + 1 : 2 * heads + 2, :], 2 * BLK)
 
         def backward(h, d=d):
-            d_hop(d - 1, h).wait_recv()
-            d_hop(d, h).start()
+            if d == 1:
+                a_hop(2, h).wait_recv()
+                a_hop(3, h).start()
             delta = stats_own[pl.ds(heads + h, 1), :]
-            dscore = (s_ref[d, h] * (nt(vb[d, h], db[0, h]) - delta)).astype(BF16)
+            dscore = (s_ref[d, h] * (nt(vb[d, h], db[h]) - delta)).astype(BF16)
             dq_acc[h] += tn(dscore, kb[d, h])
+            grad_h = cotangent(
+                ab[d, h], gb[d, h], gain_rows[h, 0:1, :], rms_d[...], pull_d[...]
+            )
             log_total = stats_next[d - 1, pl.ds(h, 1), :]
             delta = stats_next[d - 1, pl.ds(heads + h, 1), :]
             weights = jnp.exp(r_ref[d - 1, h] - log_total)
-            grad_h = db[d, h]
             dv_acc[h] += nn(weights.astype(BF16), grad_h)
             dscore = (weights * (nt(vb[0, h], grad_h) - delta)).astype(BF16)
             dk_acc[h] += nn(dscore, qb[d, h])
@@ -373,16 +405,19 @@
     for h in range(heads):
         cols = slice(h * HSZ, (h + 1) * HSZ)
         delta = stats_own[heads + h : heads + h + 1, 0:BLK]
-        dscore = (s4_ref[h] * (nt(v4[h], db[0, h, 0:BLK, :]) - delta)).astype(BF16)
+        dscore = (s4_ref[h] * (nt(v4[h], db[h, 0:BLK, :]) - delta)).astype(BF16)
         dq_acc[h, 0:BLK, :] += tn(dscore, k4[h])
         dq_ref[:, cols] = (dq_acc[h] * factor).astype(BF16)
+    rms = column(stats_next[3, 2 * heads : 2 * heads + 1, 0:BLK], BLK)
+    pull = column(stats_next[3, 2 * heads + 1 : 2 * heads + 2, 0:BLK], BLK)
     for h in range(heads):
         cols = slice(h * HSZ, (h + 1) * HSZ)
-        d_hop(3, h).wait_recv()
+        g_hop(3, h).wait_recv()
+        a_hop(3, h).wait_recv()
         log_total = stats_next[3, h : h + 1, 0:BLK]
         delta = stats_next[3, heads + h : heads + h + 1, 0:BLK]
         weights = jnp.exp(r4_ref[h] - log_total)
-        grad_h = d4[h]
+        grad_h = cotangent(a4[h], g4[h], gain_rows[h, 0:1, :], rms, pull)
         dv_acc[h, BLK : 2 * BLK, :] += nn(weights.astype(BF16), grad_h)
         dscore = (weights * (nt(vb[0, h, BLK : 2 * BLK, :], grad_h) - delta)).astype(BF16)
         dk_acc[h, BLK : 2 * BLK, :] += nn(dscore, q4[h])
@@ -398,7 +433,8 @@
             k_hop(hop, h).wait_send()
             q_hop(hop, h).wait_send()
             v_hop(hop, h).wait_send()
-            d_hop(hop, h).wait_send()
+            g_hop(hop, h).wait_send()
+            a_hop(hop, h).wait_send()
     for off in range(1, n_head):
         head_copy(off).wait_send()
     for stage, (_, radix) in enumerate(stages):
@@ -427,9 +463,9 @@
     last = pltpu.VMEM((heads, BLK, HSZ), BF16)
     wide = pltpu.VMEM((heads, rows, HSZ), F32)
     dma = pltpu.SemaphoreType.DMA
-    hops = [dma((REACH, heads))] * 8 + [dma((REACH,))] * 6
+    hops = [dma((REACH, heads))] * 10 + [dma((REACH,))] * 6
     most = max(radix for _, radix in stages) - 1
-    scratch = [full] * 4 + [last] * 4
+    scratch = [full] * 5 + [last] * 5
     scratch += [
         pltpu.VMEM((heads, rows, HSZ), BF16),
         pltpu.VMEM((8, BLK), jnp.int32),
@@ -442,7 +478,6 @@
         pltpu.VMEM((REACH - 1, heads, rows, rows), F32),
         pltpu.VMEM((heads, BLK, BLK), F32),
         wide,
-        pltpu.VMEM((heads, rows, HSZ), BF16),
         pltpu.VMEM((8, rows), F32),
         pltpu.VMEM((n_head - 1, 8, rows), F32),
         pltpu.VMEM((len(stages) + 1, 8, HSZ), F32),
@@ -450,6 +485,9 @@
         wide,
         wide,
         wide,
+        pltpu.VMEM((heads, 8, HSZ), F32),
+        pltpu.VMEM((rows, HSZ), F32),
+        pltpu.VMEM((rows, HSZ), F32),
         dma((4, heads)),
     ]
     scratch += hops

time: 84.4 us -> 86.2 us (1.021)
  the two profiles are of different devices: /device:TPU:6 before, /device:TPU:64 now
where the time goes in v3:
time: 86.2 us; the launch traced here: 86.1 us
  Pallas kernels  85.4 us (99%)
    pallas_call x1, Pallas kernels, body(): pl.pallas_call(functools.partial(kernel, n_tm, n_head, heads, stages), ou...  82.7 us
    pallas_call x1, Pallas kernels, body(): pl.pallas_call(put_out, out_shape=[big] * 4 + [jax.ShapeDtypeStruct((widt...  2.69 us

profile of v3, /device:TPU:64, one launch (start us, length us, event | category | flops | bytes accessed | tf_op | source)
XLA Modules:
  0.0 86.1 jit_solution(3210095785606631734)
XLA Ops:
  0.6 82.7 %attention_step.1 = (bf16[256,384]{1,0:T(8,128)(2,1)}, bf16[256,384]{1,0:T(8,128)(2,1)}, bf16[256,384]{1,0:T(8,128)(2,1)}, bf16[256,384]{1,0:T(8,128)(2,1)}, f32[1,384]{1,0:T(1,128)}) custom-call(bf16[256,384]{1,0:T(8,128)(2,1)} %q_hbm.1, bf16[256,384]{1,0:T(8,128)(2,1)} %k_hbm.1, bf16[256,384]{1,0:T(8,128)(2,1)} %v_hbm.1, bf16[256,384]{1,0:T(8,128)(2,1)} %g_hbm.1, ...), custom_call_target="tpu_custom_call" | custom-call | tf_op jit(solution)/shard_map/attention_step/pallas_call | solution.py:498
  83.4 2.7 %put_out.1 = (bf16[256,384]{1,0:T(8,128)(2,1)}, bf16[256,384]{1,0:T(8,128)(2,1)}, bf16[256,384]{1,0:T(8,128)(2,1)}, bf16[256,384]{1,0:T(8,128)(2,1)}, f32[384]{0:T(512)}) custom-call(bf16[256,384]{1,0:T(8,128)(2,1)} %get-tuple-element.10.refs_0_, bf16[256,384]{1,0:T(8,128)(2,1)} %get-tuple-element.11.refs_1_, bf16[256,384]{1,0:T(8,128)(2,1)} %get-tuple-element.12.refs_2_, ...), custom_call_target="tpu_custom_call" | custom-call | tf_op jit(solution)/shard_map/put_out/pallas_call | solution.py:508

commit v4 on v3

--- a/solution.py
+++ b/solution.py
@@ -297,6 +297,9 @@
 
     for off in range(1, n_head):
         head_copy(off).start()
+    for h in range(heads):
+        a_hop(0, h).wait_recv()
+        a_hop(1, h).start()
     sums = sums_own[...]
     for off in range(1, n_head):
         head_copy(off).wait_recv()
@@ -324,8 +327,8 @@
     st_hop(0).start()
     gain_own[...] = jnp.zeros(gain_own.shape, F32)
     for h in range(heads):
-        a_hop(0, h).wait_recv()
-        a_hop(1, h).start()
+        a_hop(1, h).wait_recv()
+        a_hop(2, h).start()
         cols = slice(h * HSZ, (h + 1) * HSZ)
         scaled_att = ab[0, h].astype(F32) * rms
         normed_ref[:, cols] = (scaled_att * gain_ref[cols].reshape(1, HSZ)).astype(BF16)
@@ -356,8 +359,6 @@
     gain_begin(0)
 
     def own_block(h):
-        a_hop(1, h).wait_recv()
-        a_hop(2, h).start()
         weights = s_ref[0, h]
         grad_h = db[h]
         delta = stats_own[pl.ds(heads + h, 1), :]
@@ -367,6 +368,9 @@
         dv_acc[h] = nn(weights.astype(BF16), grad_h)
 
     over_heads(own_block)
+    for h in range(heads):
+        a_hop(2, h).wait_recv()
+        a_hop(3, h).start()
 
     for h in range(heads):
         cols = slice(h * HSZ, (h + 1) * HSZ)
@@ -379,9 +383,6 @@
         pull_d[...] = column(stats_next[d - 1, 2 * heads + 1 : 2 * heads + 2, :], 2 * BLK)
 
         def backward(h, d=d):
-            if d == 1:
-                a_hop(2, h).wait_recv()
-                a_hop(3, h).start()
             delta = stats_own[pl.ds(heads + h, 1), :]
             dscore = (s_ref[d, h] * (nt(vb[d, h], db[h]) - delta)).astype(BF16)
             dq_acc[h] += tn(dscore, kb[d, h])

time: 86.2 us -> 84.3 us (0.978)
  the two profiles are of different devices: /device:TPU:64 before, /device:TPU:6 now
where the time goes in v4:
time: 84.3 us; the launch traced here: 83.2 us
  Pallas kernels  82.5 us (98%)
    pallas_call x1, Pallas kernels, body(): pl.pallas_call(functools.partial(kernel, n_tm, n_head, heads, stages), ou...  79.9 us
    pallas_call x1, Pallas kernels, body(): pl.pallas_call(put_out, out_shape=[big] * 4 + [jax.ShapeDtypeStruct((widt...  2.69 us

profile of v4, /device:TPU:6, one launch (start us, length us, event | category | flops | bytes accessed | tf_op | source)
XLA Modules:
  0.0 83.2 jit_solution(6611172892836244820)
XLA Ops:
  0.6 79.9 %attention_step.1 = (bf16[256,384]{1,0:T(8,128)(2,1)}, bf16[256,384]{1,0:T(8,128)(2,1)}, bf16[256,384]{1,0:T(8,128)(2,1)}, bf16[256,384]{1,0:T(8,128)(2,1)}, f32[1,384]{1,0:T(1,128)}) custom-call(bf16[256,384]{1,0:T(8,128)(2,1)} %q_hbm.1, bf16[256,384]{1,0:T(8,128)(2,1)} %k_hbm.1, bf16[256,384]{1,0:T(8,128)(2,1)} %v_hbm.1, bf16[256,384]{1,0:T(8,128)(2,1)} %g_hbm.1, ...), custom_call_target="tpu_custom_call" | custom-call | tf_op jit(solution)/shard_map/attention_step/pallas_call | solution.py:499
  80.5 2.7 %put_out.1 = (bf16[256,384]{1,0:T(8,128)(2,1)}, bf16[256,384]{1,0:T(8,128)(2,1)}, bf16[256,384]{1,0:T(8,128)(2,1)}, bf16[256,384]{1,0:T(8,128)(2,1)}, f32[384]{0:T(512)}) custom-call(bf16[256,384]{1,0:T(8,128)(2,1)} %get-tuple-element.10.refs_0_, bf16[256,384]{1,0:T(8,128)(2,1)} %get-tuple-element.11.refs_1_, bf16[256,384]{1,0:T(8,128)(2,1)} %get-tuple-element.12.refs_2_, ...), custom_call_target="tpu_custom_call" | custom-call | tf_op jit(solution)/shard_map/put_out/pallas_call | solution.py:509

commit v5 on v4

--- a/solution.py
+++ b/solution.py
@@ -69,6 +69,8 @@
     ids_next,
     stats_own,
     stats_next,
+    ls_own,
+    ls_next,
     s_ref,
     s4_ref,
     r_ref,
@@ -101,6 +103,8 @@
     in_recv,
     st_send,
     st_recv,
+    ls_send,
+    ls_recv,
     hd_send,
     hd_recv,
     gn_send,
@@ -174,6 +178,7 @@
 
     ip_hop = functools.partial(small_hop, ids_own, ids_prev, ip_send, ip_recv, later)
     in_hop = functools.partial(small_hop, ids_own, ids_next, in_send, in_recv, earlier)
+    ls_hop = functools.partial(small_hop, ls_own, ls_next, ls_send, ls_recv, earlier)
     st_hop = functools.partial(small_hop, stats_own, stats_next, st_send, st_recv, earlier)
 
     def over_heads(step):
@@ -253,13 +258,17 @@
         for d in range(REACH):
             s_ref[d, h] = s_ref[d, h] * inverse
         s4_ref[h] = e4 * inverse[:, 0:BLK]
-        stats_own[pl.ds(h, 1), :] = top + jnp.log(total)
+        ls_own[pl.ds(h, 1), :] = top + jnp.log(total)
         out_acc[h] = tn(s_ref[0, h].astype(BF16), vb[0, h])
 
     stats_own[...] = jnp.zeros(stats_own.shape, F32)
+    ls_own[...] = jnp.zeros(ls_own.shape, F32)
     over_heads(soften)
+    ls_hop(0).start()
 
     for d in range(1, REACH):
+        ls_hop(d - 1).wait_recv()
+        ls_hop(d).start()
 
         def attend(h, d=d):
             v_hop(d - 1, h).wait_recv()
@@ -267,6 +276,7 @@
             g_hop(d - 1, h).wait_recv()
             g_hop(d, h).start()
             out_acc[h] += tn(s_ref[d, h].astype(BF16), vb[d, h])
+            r_ref[d - 1, h] = jnp.exp(r_ref[d - 1, h] - ls_next[d - 1, pl.ds(h, 1), :])
 
         over_heads(attend)
 
@@ -297,7 +307,9 @@
 
     for off in range(1, n_head):
         head_copy(off).start()
-    for h in range(heads):
+    ls_hop(3).wait_recv()
+    for h in range(heads):
+        r4_ref[h] = jnp.exp(r4_ref[h] - ls_next[3, h : h + 1, 0:BLK])
         a_hop(0, h).wait_recv()
         a_hop(1, h).start()
     sums = sums_own[...]
@@ -368,9 +380,6 @@
         dv_acc[h] = nn(weights.astype(BF16), grad_h)
 
     over_heads(own_block)
-    for h in range(heads):
-        a_hop(2, h).wait_recv()
-        a_hop(3, h).start()
 
     for h in range(heads):
         cols = slice(h * HSZ, (h + 1) * HSZ)
@@ -383,15 +392,17 @@
         pull_d[...] = column(stats_next[d - 1, 2 * heads + 1 : 2 * heads + 2, :], 2 * BLK)
 
         def backward(h, d=d):
+            if d == 1:
+                a_hop(2, h).wait_recv()
+                a_hop(3, h).start()
             delta = stats_own[pl.ds(heads + h, 1), :]
             dscore = (s_ref[d, h] * (nt(vb[d, h], db[h]) - delta)).astype(BF16)
             dq_acc[h] += tn(dscore, kb[d, h])
             grad_h = cotangent(
                 ab[d, h], gb[d, h], gain_rows[h, 0:1, :], rms_d[...], pull_d[...]
             )
-            log_total = stats_next[d - 1, pl.ds(h, 1), :]
             delta = stats_next[d - 1, pl.ds(heads + h, 1), :]
-            weights = jnp.exp(r_ref[d - 1, h] - log_total)
+            weights = r_ref[d - 1, h]
             dv_acc[h] += nn(weights.astype(BF16), grad_h)
             dscore = (weights * (nt(vb[0, h], grad_h) - delta)).astype(BF16)
             dk_acc[h] += nn(dscore, qb[d, h])
@@ -415,9 +426,8 @@
         cols = slice(h * HSZ, (h + 1) * HSZ)
         g_hop(3, h).wait_recv()
         a_hop(3, h).wait_recv()
-        log_total = stats_next[3, h : h + 1, 0:BLK]
         delta = stats_next[3, heads + h : heads + h + 1, 0:BLK]
-        weights = jnp.exp(r4_ref[h] - log_total)
+        weights = r4_ref[h]
         grad_h = cotangent(a4[h], g4[h], gain_rows[h, 0:1, :], rms, pull)
         dv_acc[h, BLK : 2 * BLK, :] += nn(weights.astype(BF16), grad_h)
         dscore = (weights * (nt(vb[0, h, BLK : 2 * BLK, :], grad_h) - delta)).astype(BF16)
@@ -430,6 +440,7 @@
         ip_hop(hop).wait_send()
         in_hop(hop).wait_send()
         st_hop(hop).wait_send()
+        ls_hop(hop).wait_send()
         for h in range(heads):
             k_hop(hop, h).wait_send()
             q_hop(hop, h).wait_send()
@@ -464,7 +475,7 @@
     last = pltpu.VMEM((heads, BLK, HSZ), BF16)
     wide = pltpu.VMEM((heads, rows, HSZ), F32)
     dma = pltpu.SemaphoreType.DMA
-    hops = [dma((REACH, heads))] * 10 + [dma((REACH,))] * 6
+    hops = [dma((REACH, heads))] * 10 + [dma((REACH,))] * 8
     most = max(radix for _, radix in stages) - 1
     scratch = [full] * 5 + [last] * 5
     scratch += [
@@ -472,6 +483,8 @@
         pltpu.VMEM((8, BLK), jnp.int32),
         pltpu.VMEM((REACH, 8, BLK), jnp.int32),
         pltpu.VMEM((REACH, 8, BLK), jnp.int32),
+        pltpu.VMEM((8, rows), F32),
+        pltpu.VMEM((REACH, 8, rows), F32),
         pltpu.VMEM((8, rows), F32),
         pltpu.VMEM((REACH, 8, rows), F32),
         pltpu.VMEM((REACH, heads, rows, rows), F32),

time: 84.3 us -> 86.2 us (1.023); the launches traced: 83.2 us -> 86 us
  Pallas kernels: 82.5 us -> 85.4 us
    pallas_call x1, Pallas kernels: 79.9 us -> 82.7 us  [body(): pl.pallas_call(functools.partial(kernel, n_tm, n_head, heads, stages), ou...]
where the time goes in v5:
time: 86.2 us; the launch traced here: 86 us
  Pallas kernels  85.4 us (99%)
    pallas_call x1, Pallas kernels, body(): pl.pallas_call(functools.partial(kernel, n_tm, n_head, heads, stages), ou...  82.7 us
    pallas_call x1, Pallas kernels, body(): pl.pallas_call(put_out, out_shape=[big] * 4 + [jax.ShapeDtypeStruct((widt...  2.69 us

profile of v5, /device:TPU:6, one launch (start us, length us, event | category | flops | bytes accessed | tf_op | source)
XLA Modules:
  0.0 86.0 jit_solution(8071852316244562560)
XLA Ops:
  0.6 82.7 %attention_step.1 = (bf16[256,384]{1,0:T(8,128)(2,1)}, bf16[256,384]{1,0:T(8,128)(2,1)}, bf16[256,384]{1,0:T(8,128)(2,1)}, bf16[256,384]{1,0:T(8,128)(2,1)}, f32[1,384]{1,0:T(1,128)}) custom-call(bf16[256,384]{1,0:T(8,128)(2,1)} %q_hbm.1, bf16[256,384]{1,0:T(8,128)(2,1)} %k_hbm.1, bf16[256,384]{1,0:T(8,128)(2,1)} %v_hbm.1, bf16[256,384]{1,0:T(8,128)(2,1)} %g_hbm.1, ...), custom_call_target="tpu_custom_call" | custom-call | tf_op jit(solution)/shard_map/attention_step/pallas_call | solution.py:512
  83.3 2.7 %put_out.1 = (bf16[256,384]{1,0:T(8,128)(2,1)}, bf16[256,384]{1,0:T(8,128)(2,1)}, bf16[256,384]{1,0:T(8,128)(2,1)}, bf16[256,384]{1,0:T(8,128)(2,1)}, f32[384]{0:T(512)}) custom-call(bf16[256,384]{1,0:T(8,128)(2,1)} %get-tuple-element.10.refs_0_, bf16[256,384]{1,0:T(8,128)(2,1)} %get-tuple-element.11.refs_1_, bf16[256,384]{1,0:T(8,128)(2,1)} %get-tuple-element.12.refs_2_, ...), custom_call_target="tpu_custom_call" | custom-call | tf_op jit(solution)/shard_map/put_out/pallas_call | solution.py:522

commit v6 on v3

--- a/solution.py
+++ b/solution.py
@@ -297,6 +297,9 @@
 
     for off in range(1, n_head):
         head_copy(off).start()
+    for h in range(heads):
+        a_hop(0, h).wait_recv()
+        a_hop(1, h).start()
     sums = sums_own[...]
     for off in range(1, n_head):
         head_copy(off).wait_recv()
@@ -324,8 +327,6 @@
     st_hop(0).start()
     gain_own[...] = jnp.zeros(gain_own.shape, F32)
     for h in range(heads):
-        a_hop(0, h).wait_recv()
-        a_hop(1, h).start()
         cols = slice(h * HSZ, (h + 1) * HSZ)
         scaled_att = ab[0, h].astype(F32) * rms
         normed_ref[:, cols] = (scaled_att * gain_ref[cols].reshape(1, HSZ)).astype(BF16)

time: 86.2 us -> 83.2 us (0.965)
  the two profiles are of different devices: /device:TPU:64 before, /device:TPU:6 now
where the time goes in v6:
time: 83.2 us; the launch traced here: 82 us
  Pallas kernels  81.3 us (98%)
    pallas_call x1, Pallas kernels, body(): pl.pallas_call(functools.partial(kernel, n_tm, n_head, heads, stages), ou...  78.6 us
    pallas_call x1, Pallas kernels, body(): pl.pallas_call(put_out, out_shape=[big] * 4 + [jax.ShapeDtypeStruct((widt...  2.69 us

profile of v6, /device:TPU:6, one launch (start us, length us, event | category | flops | bytes accessed | tf_op | source)
XLA Modules:
  0.0 82.0 jit_solution(13537349591748533252)
XLA Ops:
  0.6 78.6 %attention_step.1 = (bf16[256,384]{1,0:T(8,128)(2,1)}, bf16[256,384]{1,0:T(8,128)(2,1)}, bf16[256,384]{1,0:T(8,128)(2,1)}, bf16[256,384]{1,0:T(8,128)(2,1)}, f32[1,384]{1,0:T(1,128)}) custom-call(bf16[256,384]{1,0:T(8,128)(2,1)} %q_hbm.1, bf16[256,384]{1,0:T(8,128)(2,1)} %k_hbm.1, bf16[256,384]{1,0:T(8,128)(2,1)} %v_hbm.1, bf16[256,384]{1,0:T(8,128)(2,1)} %g_hbm.1, ...), custom_call_target="tpu_custom_call" | custom-call | tf_op jit(solution)/shard_map/attention_step/pallas_call | solution.py:499
  79.3 2.7 %put_out.1 = (bf16[256,384]{1,0:T(8,128)(2,1)}, bf16[256,384]{1,0:T(8,128)(2,1)}, bf16[256,384]{1,0:T(8,128)(2,1)}, bf16[256,384]{1,0:T(8,128)(2,1)}, f32[384]{0:T(512)}) custom-call(bf16[256,384]{1,0:T(8,128)(2,1)} %get-tuple-element.10.refs_0_, bf16[256,384]{1,0:T(8,128)(2,1)} %get-tuple-element.11.refs_1_, bf16[256,384]{1,0:T(8,128)(2,1)} %get-tuple-element.12.refs_2_, ...), custom_call_target="tpu_custom_call" | custom-call | tf_op jit(solution)/shard_map/put_out/pallas_call | solution.py:509
